TPU v7x, 256 devices: a whole 4x4x8 slice. The times are simulated.
256 devices in a mesh: cuts: 16 (over z_lo, y, core), col: 16 (over z_hi, x).
Axes of the slice: x: 4, y: 4, z: 8 (z_hi: 4, z_lo: 2; z = z_hi * 2 + z_lo), core: 2. Of those that a mesh axis runs over, the one named last changes fastest.
Arguments:
- data: bfloat16 [16, 64, 64, 1024], P('cuts', None, 'col'), may hold values from -12 to 12
- weights: float32 [16, 64], replicated, may hold values from 0.5 to 2
- mixing: float32 [64, 64], replicated, may hold values from -0.4 to 2.9
Outputs:
- factor: float32 [64, 64, 1024], P(None, 'col')
- updated: float32 [16, 64], P('cuts')
All inputs are finite; a program needn't handle non-finite values.
Results may differ from a plain program's by a relative error of at most 0.0029.
Values sent between devices are 32-bit elements; how exact they have to be, the bound alone decides.
A program may use at most 64 MiB of HBM per device.

v0:
```python
import jax
import jax.numpy as jnp
from jax import lax
from jax.sharding import PartitionSpec as P

GRID = 32
ITERS = 3
strength = 0.5
highest = lax.Precision.HIGHEST
low_edge = 1.0
high_edge = 1.0 + 12.0 * strength
centre = (high_edge + low_edge) / 2.0
spread = (high_edge - low_edge) / 2.0


def extended_2(cells, sides, width):
    for axis, dim in sides:
        count = lax.axis_size(axis)
        ends = count - 1
        head = lax.slice_in_dim(cells, 0, width, axis=dim)
        tail = lax.slice_in_dim(cells, cells.shape[dim] - width, cells.shape[dim], axis=dim)
        cells = jnp.concatenate(
            [
                lax.ppermute(tail, axis, [(i, (i + 1) % count) for i in range(ends)]),
                cells,
                lax.ppermute(head, axis, [((i + 1) % count, i) for i in range(ends)]),
            ],
            axis=dim,
        )
    return cells


def split_up(shard, dim, devices):
    before, after = (shard.shape[:dim], shard.shape[dim + 1 :])
    return jnp.moveaxis(shard.reshape(*before, devices, -1, *after), dim, 0)


def sent_and_summed(shard, axis, dim):
    tiles = split_up(shard, dim, lax.axis_size(axis))
    arrived = lax.all_to_all(tiles, axis, split_axis=0, concat_axis=0, tiled=True)
    return arrived.sum(axis=0)


def joined_along(tiles, dim):
    dims = list(tiles.shape[1:])
    dims[dim] *= tiles.shape[0]
    return jnp.moveaxis(tiles, 0, dim).reshape(dims)


def from_everyone(shard, axis):
    devices = lax.axis_size(axis)
    return lax.all_to_all(
        jnp.broadcast_to(shard[None], (devices, *shard.shape)), axis, 0, 0, tiled=True
    )


def gather_directly(shard, axis, dim):
    return joined_along(from_everyone(shard, axis), dim)


def taken_together(shard, axis):
    return from_everyone(shard, axis).sum(axis=0)


def packed_total(arrays, axis):
    line, at, done = (jnp.concatenate([a.reshape(-1) for a in arrays]), 0, [])
    running = taken_together(line, axis)
    for a in arrays:
        done.append(running[at : at + a.size].reshape(a.shape))
        at += a.size
    return tuple(done)


def operate(extended):
    channels, depth, cells = extended.shape
    edge = GRID
    interior = extended[:, 1:-1]
    column = jnp.arange(cells, dtype=jnp.int32) % edge
    has_left = (column > 0).astype(jnp.float32)
    has_right = (column < edge - 1).astype(jnp.float32)
    left_part = jnp.pad(interior, ((0, 0), (0, 0), (1, 0)))[:, :, :-1] * has_left
    right_part = jnp.pad(interior, ((0, 0), (0, 0), (0, 1)))[:, :, 1:] * has_right
    upper_part = jnp.pad(interior, ((0, 0), (0, 0), (edge, 0)))[:, :, :-edge]
    lower_part = jnp.pad(interior, ((0, 0), (0, 0), (0, edge)))[:, :, edge:]
    neighbours = extended[:, 2:] + extended[:, :-2]
    neighbours = neighbours + left_part + right_part + upper_part + lower_part
    return interior + strength * (6.0 * interior - neighbours)


def smooth_once(source):
    planes = source.shape[1]
    extended = extended_2(source, (("col", 1),), ITERS)
    first_plane = lax.axis_index("col") * planes - ITERS
    total_planes = planes * lax.axis_size("col")
    levels = first_plane + jnp.arange(planes + 2 * ITERS, dtype=jnp.int32)
    inside = ((levels >= 0) & (levels < total_planes)).astype(jnp.float32)[None, :, None]
    solution = jnp.zeros_like(source)
    residual = extended
    direction = extended / centre
    ratio = spread / centre
    for iteration in range(ITERS):
        margin = ITERS - iteration
        solution = solution + direction[:, margin : margin + planes]
        window = inside[:, iteration + 1 : iteration + 1 + planes + 2 * (margin - 1)]
        residual = (residual[:, 1:-1] - operate(direction)) * window
        ratio_next = 1.0 / (2.0 * centre / spread - ratio)
        direction = ratio_next * ratio * direction[:, 1:-1] + 2.0 * ratio_next / spread * residual
        ratio = ratio_next
    return solution + direction


def smooth(source):
    return smooth_once(source)


def per_device(data, weights, mixing):
    local_scans, ranks, planes, cells = data.shape
    mix_gram = jnp.dot(mixing.T, mixing, precision=highest)
    weight_gram = jnp.dot(weights.T, weights, precision=highest)
    lower_factor = jnp.linalg.cholesky(mix_gram * weight_gram)
    own_weights = lax.dynamic_slice_in_dim(
        weights, lax.axis_index("cuts") * local_scans, local_scans, 0
    )
    scaled = (mixing[None, :, :] * own_weights[:, None, :]).reshape(local_scans * ranks, ranks)
    coefficients = jax.scipy.linalg.cho_solve((lower_factor, True), scaled.T).T.astype(jnp.bfloat16)
    stacked = data.reshape(local_scans * ranks, planes * cells)
    portion = lax.psum_scatter(
        lax.dot_general(
            coefficients, stacked, (((0,), (0,)), ((), ())), preferred_element_type=jnp.float32
        ),
        "cuts",
        scatter_dimension=0,
        tiled=True,
    )
    smoothed = smooth(portion.reshape(-1, planes, cells))
    factor = lax.all_gather(smoothed, "cuts", axis=0, tiled=True)
    factor_flat = factor.reshape(ranks, planes * cells)
    factor_half = factor_flat.astype(jnp.bfloat16)
    factor_gram = jnp.dot(factor_flat, factor_flat.T, precision=highest)
    products = lax.dot_general(
        data.reshape(local_scans, ranks, planes * cells),
        factor_half,
        (((2,), (1,)), ((), ())),
        preferred_element_type=jnp.float32,
    )
    targets = jnp.sum(mixing[None, :, :] * products, axis=1)
    factor_gram, targets = lax.psum((factor_gram, targets), "col")
    lower_next = jnp.linalg.cholesky(mix_gram * factor_gram)
    updated = jax.scipy.linalg.cho_solve((lower_next, True), targets.T).T
    return (factor, updated)


def solution(mesh):
    return jax.shard_map(
        per_device,
        mesh=mesh,
        in_specs=(P("cuts", None, "col", None), P(), P()),
        out_specs=(P(None, "col", None), P("cuts", None)),
        check_vma=False,
    )
```

profile of v0, /device:TPU:8, one launch (start us, length us, event | category | flops | bytes accessed | tf_op | source)
XLA Modules:
  0.0 309.4 jit_solution(8941545026422105702)
XLA Ops:
  7.2 0.0 copy-start
  7.2 0.0 all-reduce.16.cloned.1.call-start
  7.2 1.1 fusion.60
  8.3 0.2 convolution_multiply_fusion
  8.6 0.1 copy.28
  8.7 5.8 %cholesky.44 = f32[64,64]{1,0:T(8,128)S(1)} custom-call(f32[64,64]{1,0:T(8,128)S(1)} %fusion.46), custom_call_target="Cholesky" | custom-call | tf_op jit(solution)/shard_map/jit(cholesky)/cholesky | solution.py:120
  14.5 0.6 compare_reduce_fusion.1
  15.2 0.7 fusion.37
  15.8 4.9 %custom-call.16 = f32[1,64,64]{1,2,0:T(8,128)S(1)} custom-call(f32[1,64,64]{2,1,0:T(8,128)S(1)} %fusion.37), custom_call_target="InvertDiagBlocksLowerTriangular" | custom-call | tf_op jit(solution)/shard_map/jit(_cho_solve)/triangular_solve | solution.py:125
  20.8 0.2 fusion.44
  21.0 0.2 convolution_convert_fusion
  21.3 1.2 copy.38
  22.5 1.3 fusion.61
  23.8 0.0 all-reduce.16.cloned.1.call-update
  23.8 0.0 all-gather.2.cloned.1.call-start
  23.8 0.0 copy-start.3
  23.9 0.7 copy-done.3
  24.5 0.6 dynamic-slice
  25.8 0.1 slice_bitcast_fusion.2
  25.9 0.1 slice_bitcast_fusion.1
  25.9 0.1 slice_bitcast_fusion
  26.0 122.3 %all-reduce.16.cloned.1.call-done = f32[64,4096]{1,0:T(8,128)} async-done(((f32[64,4096]{1,0:T(8,128)}), f32[64,4096]{1,0:T(8,128)}) %all-reduce.16.cloned.1.call-update) | async-done | bytes 1048592
  148.3 0.9 constant_dynamic-slice_fusion
  149.2 0.1 reshape.87
  149.3 3.1 %collective-permute-start = (f32[4,3,1024]{2,1,0:T(4,128)S(1)}, f32[4,3,1024]{2,1,0:T(4,128)S(1)}, u32[]{:S(2)}, u32[]{:S(2)}) collective-permute-start(f32[4,3,1024]{2,1,0:T(4,128)S(1)} %get-tuple-element.15), channel_id=1, source_target_pairs={{0,1},{1,2},{2,3},{3,4},{4,5},{5,6},{6,7},{7,8},{8,9},{9,10},{10,1... | collective-permute-start | bytes 147464 | tf_op jit(solution)/shard_map/ppermute | solution.py:24
  152.4 1.3 collective-permute-start.1
  153.7 0.6 collective-permute-done
  154.3 4.3 %collective-permute-done.1 = f32[4,3,1024]{2,1,0:T(4,128)S(1)} collective-permute-done((f32[4,3,1024]{2,1,0:T(4,128)S(1)}, f32[4,3,1024]{2,1,0:T(4,128)S(1)}, u32[]{:S(2)}, u32[]{:S(2)}) %collective-permute-start.1) | collective-permute-done | bytes 49184 | tf_op jit(solution)/shard_map/ppermute | solution.py:26
  158.6 0.1 pad_maximum_fusion
  158.7 0.2 multiply_add_fusion.1
  158.9 0.2 multiply_add_fusion
  159.2 0.9 fusion.36
  160.0 0.0 all-gather.2.cloned.1.call-update
  160.1 41.6 %all-gather.2.cloned.1.call-done = f32[64,4,1024]{2,1,0:T(4,128)} async-done(((f32[4,4,1024]{2,1,0:T(4,128)}), f32[64,4,1024]{2,1,0:T(4,128)}) %all-gather.2.cloned.1.call-update) | async-done | bytes 1048592 | tf_op jit(solution)/shard_map/all_gather | solution.py:136
  201.6 1.4 convert_element_type.73
  203.1 0.2 copy.39
  203.2 0.3 fusion.1
  203.5 0.7 copy-done.1
  204.3 2.0 convolution_bitcast_fusion.1
  206.3 82.2 %all-reduce.13 = (f32[64,64]{0,1:T(8,128)S(1)}, f32[64]{0:T(128)S(1)}) all-reduce(f32[64,64]{0,1:T(8,128)S(1)} %convolution_bitcast_fusion.1, f32[64]{0:T(128)S(1)} %fusion.1), channel_id=1, replica_groups=mesh['cuts'=16,'col'=16] {'col'}, use_global_device_ids=true, to_apply=%region_3.5 | all-reduce | flops 4160 | bytes 33280 | tf_op jit(solution)/shard_map/psum | solution.py:147
  288.5 0.1 copy.33
  288.6 5.8 %cholesky.55 = f32[64,64]{1,0:T(8,128)S(1)} custom-call(f32[64,64]{1,0:T(8,128)S(1)} %fusion.42), custom_call_target="Cholesky" | custom-call | tf_op jit(solution)/shard_map/jit(cholesky)/cholesky | solution.py:148
  294.5 0.6 compare_reduce_fusion
  295.1 0.7 fusion.38
  295.8 4.9 %custom-call.17 = f32[1,64,64]{1,2,0:T(8,128)S(1)} custom-call(f32[1,64,64]{2,1,0:T(8,128)S(1)} %fusion.38), custom_call_target="InvertDiagBlocksLowerTriangular" | custom-call | tf_op jit(solution)/shard_map/jit(_cho_solve)/triangular_solve | solution.py:149
  300.7 0.2 convolution_bitcast_fusion.2
  300.9 0.7 fusion.39
  301.6 1.0 copy.44
  (16 shorter events, 0.2 us)
Async XLA Ops:
  7.2 1.1 copy-start
  7.2 141.1 %all-reduce.16.cloned.1.call-start = ((), (), s32[]{:S(2)}) async-start(), calls=%async_computation.1 | async-start | bytes 2097152
  15.2 5.6 %copy-start.2 = (f32[64,64]{1,0:T(8,128)S(1)}, f32[64,64]{1,0:T(8,128)}, u32[]{:S(2)}) copy-start(f32[64,64]{1,0:T(8,128)} %param.6) | copy-start | bytes 49156
  23.8 177.8 %all-gather.2.cloned.1.call-start = ((), (), s32[]{:S(2)}) async-start(), calls=%async_computation | async-start | bytes 1114112 | tf_op jit(solution)/shard_map/all_gather | solution.py:136
  23.8 0.7 copy-start.3
  149.3 5.0 %collective-permute-start = (f32[4,3,1024]{2,1,0:T(4,128)S(1)}, f32[4,3,1024]{2,1,0:T(4,128)S(1)}, u32[]{:S(2)}, u32[]{:S(2)}) collective-permute-start(f32[4,3,1024]{2,1,0:T(4,128)S(1)} %get-tuple-element.15), channel_id=1, source_target_pairs={{0,1},{1,2},{2,3},{3,4},{4,5},{5,6},{6,7},{7,8},{8,9},{9,10},{10,1... | collective-permute-start | bytes 147464 | tf_op jit(solution)/shard_map/ppermute | solution.py:24
  152.4 6.2 %collective-permute-start.1 = (f32[4,3,1024]{2,1,0:T(4,128)S(1)}, f32[4,3,1024]{2,1,0:T(4,128)S(1)}, u32[]{:S(2)}, u32[]{:S(2)}) collective-permute-start(f32[4,3,1024]{2,1,0:T(4,128)S(1)} %get-tuple-element.16), channel_id=1, source_target_pairs={{1,0},{2,1},{3,2},{4,3},{5,4},{6,5},{7,6},{8,7},{9,8},{10,9},{11,1... | collective-permute-start | bytes 147464 | tf_op jit(solution)/shard_map/ppermute | solution.py:26
  203.1 1.2 copy-start.1
Sparse Core Ops, SparseCore 0:
  23.9 124.2 all-reduce.15
  160.2 41.4 all-gather.1
where the time goes:
time: 310 us; the launch traced here: 309 us
  waiting for transfers between devices  169 us (55%)
  blocking collectives  82.2 us (27%)
  other arithmetic  27 us (9%)
  between operations  14.9 us (5%)
  matrix products  6.26 us (2%)
  local copies, waits for them, and re-layouts  5.8 us (2%)
  starting transfers between devices  4.5 us (1%)
    unnamed x3, waiting for transfers between devices  122 us
    psum x1, blocking collectives, per_device(): factor_gram, targets = lax.psum((factor_gram, targets), 'col')  82.2 us
    all_gather x1, waiting for transfers between devices, per_device(): factor = lax.all_gather(smoothed, 'cuts', axis=0, tiled=True)  41.6 us
    another operation x3, other arithmetic, per_device(): lower_factor = jnp.linalg.cholesky(mix_gram * weight_gram)  6.52 us
    another operation x3, other arithmetic, per_device(): lower_next = jnp.linalg.cholesky(mix_gram * factor_gram)  6.52 us
  transfers between devices with their start and end apart: 4, of which 4 were waited for; matrix products, arithmetic and copies ran while one was open for 0% of the time, Pallas kernels for 0%

commit v1 on v0

--- a/solution.py
+++ b/solution.py
@@ -133,7 +133,9 @@
         tiled=True,
     )
     smoothed = smooth(portion.reshape(-1, planes, cells))
-    factor = lax.all_gather(smoothed, "cuts", axis=0, tiled=True)
+    factor = jnp.concatenate(
+        lax.all_to_all(jnp.stack([smoothed] * lax.axis_size("cuts")), "cuts", 0, 0), axis=0
+    )
     factor_flat = factor.reshape(ranks, planes * cells)
     factor_half = factor_flat.astype(jnp.bfloat16)
     factor_gram = jnp.dot(factor_flat, factor_flat.T, precision=highest)

time: 310 us -> 291 us (0.939)
  the two profiles are of different devices: /device:TPU:8 before, /device:TPU:128 now
where the time goes in v1:
time: 291 us; the launch traced here: 290 us
  waiting for transfers between devices  126 us (43%)
  blocking collectives  103 us (35%)
  other arithmetic  25.1 us (9%)
  between operations  14.9 us (5%)
  starting transfers between devices  10.1 us (3%)
  local copies, waits for them, and re-layouts  5.9 us (2%)
  matrix products  5.19 us (2%)
    unnamed x2, waiting for transfers between devices  124 us
    psum x1, blocking collectives, per_device(): factor_gram, targets = lax.psum((factor_gram, targets), 'col')  83.2 us
    all_to_all x1, blocking collectives, per_device(): lax.all_to_all(jnp.stack([smoothed] * lax.axis_size('cuts')), 'cuts', 0, 0)  19.7 us
    ppermute x1, starting transfers between devices, extended_2(): lax.ppermute(head, axis, [((i + 1) % count, i) for i in range(ends)])  6.69 us
    another operation x3, other arithmetic, per_device(): lower_factor = jnp.linalg.cholesky(mix_gram * weight_gram)  6.52 us
    another operation x3, other arithmetic, per_device(): lower_next = jnp.linalg.cholesky(mix_gram * factor_gram)  6.52 us
  transfers between devices with their start and end apart: 3, of which 3 were waited for; matrix products, arithmetic and copies ran while one was open for 0% of the time, Pallas kernels for 0%

profile of v1, /device:TPU:128, one launch (start us, length us, event | category | flops | bytes accessed | tf_op | source)
XLA Modules:
  0.0 290.5 jit_solution(15451912496171217994)
XLA Ops:
  7.2 0.0 copy-start
  7.2 0.0 all-reduce.16.cloned.1.call-start
  7.2 1.1 fusion.59
  8.3 0.2 convolution_multiply_fusion
  8.6 0.1 copy.13
  8.7 5.8 %cholesky.44 = f32[64,64]{1,0:T(8,128)S(1)} custom-call(f32[64,64]{1,0:T(8,128)S(1)} %fusion.45), custom_call_target="Cholesky" | custom-call | tf_op jit(solution)/shard_map/jit(cholesky)/cholesky | solution.py:120
  14.5 0.6 compare_reduce_fusion.1
  15.2 0.7 fusion.36
  15.8 4.9 %custom-call.16 = f32[1,64,64]{1,2,0:T(8,128)S(1)} custom-call(f32[1,64,64]{2,1,0:T(8,128)S(1)} %fusion.36), custom_call_target="InvertDiagBlocksLowerTriangular" | custom-call | tf_op jit(solution)/shard_map/jit(_cho_solve)/triangular_solve | solution.py:125
  20.8 0.0 copy-done.1
  20.8 0.2 fusion.43
  21.0 0.2 convolution_convert_fusion
  21.3 1.2 copy.20
  22.5 1.3 fusion.60
  23.8 0.0 all-reduce.16.cloned.1.call-update
  23.8 0.0 copy-start.2
  23.8 0.7 copy-done.2
  24.5 0.6 dynamic-slice
  25.7 0.1 slice_bitcast_fusion.2
  25.8 0.1 slice_bitcast_fusion.1
  25.9 0.1 slice_bitcast_fusion
  26.0 123.8 %all-reduce.16.cloned.1.call-done = f32[64,4096]{1,0:T(8,128)} async-done(((f32[64,4096]{1,0:T(8,128)}), f32[64,4096]{1,0:T(8,128)}) %all-reduce.16.cloned.1.call-update) | async-done | bytes 1048592
  149.8 0.9 constant_dynamic-slice_fusion
  150.7 0.1 reshape.91
  150.8 3.4 %collective-permute-start = (f32[4,3,1024]{2,1,0:T(4,128)S(1)}, f32[4,3,1024]{2,1,0:T(4,128)S(1)}, u32[]{:S(2)}, u32[]{:S(2)}) collective-permute-start(f32[4,3,1024]{2,1,0:T(4,128)S(1)} %get-tuple-element.11), channel_id=1, source_target_pairs={{0,1},{1,2},{2,3},{3,4},{4,5},{5,6},{6,7},{7,8},{8,9},{9,10},{10,1... | collective-permute-start | bytes 147464 | tf_op jit(solution)/shard_map/ppermute | solution.py:24
  154.2 6.7 %collective-permute-start.1 = (f32[4,3,1024]{2,1,0:T(4,128)S(1)}, f32[4,3,1024]{2,1,0:T(4,128)S(1)}, u32[]{:S(2)}, u32[]{:S(2)}) collective-permute-start(f32[4,3,1024]{2,1,0:T(4,128)S(1)} %get-tuple-element.12), channel_id=1, source_target_pairs={{1,0},{2,1},{3,2},{4,3},{5,4},{6,5},{7,6},{8,7},{9,8},{10,9},{11,1... | collective-permute-start | bytes 147464 | tf_op jit(solution)/shard_map/ppermute | solution.py:26
  160.9 0.4 collective-permute-done
  161.3 2.1 collective-permute-done.1
  163.4 0.1 pad_maximum_fusion
  163.5 0.2 multiply_add_fusion.1
  163.7 0.2 multiply_add_fusion
  164.0 0.2 fusion.35
  164.2 0.2 stack.2
  164.5 19.7 %all_to_all.5 = f32[16,4,4,1024]{3,2,1,0:T(4,128)S(1)} all-to-all(f32[16,4,4,1024]{3,2,1,0:T(4,128)S(1)} %stack.2), channel_id=1, replica_groups=mesh['cuts'=16,'col'=16] {'cuts'}, dimensions={0} | all-to-all | bytes 2097152 | tf_op jit(solution)/shard_map/all_to_all | solution.py:137
  184.1 0.2 convert_element_type.73
  184.3 0.2 copy.22
  184.5 0.3 fusion.1
  184.8 0.6 copy.21
  185.4 1.0 fusion.61
  186.4 83.2 %all-reduce.13 = (f32[64,64]{0,1:T(8,128)S(1)}, f32[64]{0:T(128)S(1)}) all-reduce(f32[64,64]{0,1:T(8,128)S(1)} %fusion.61, f32[64]{0:T(128)S(1)} %fusion.1), channel_id=1, replica_groups=mesh['cuts'=16,'col'=16] {'col'}, use_global_device_ids=true, to_apply=%region_3.5 | all-reduce | flops 4160 | bytes 33280 | tf_op jit(solution)/shard_map/psum | solution.py:149
  269.6 0.1 copy.16
  269.7 5.8 %cholesky.55 = f32[64,64]{1,0:T(8,128)S(1)} custom-call(f32[64,64]{1,0:T(8,128)S(1)} %fusion.41), custom_call_target="Cholesky" | custom-call | tf_op jit(solution)/shard_map/jit(cholesky)/cholesky | solution.py:150
  275.6 0.6 compare_reduce_fusion
  276.2 0.7 fusion.37
  276.9 4.9 %custom-call.17 = f32[1,64,64]{1,2,0:T(8,128)S(1)} custom-call(f32[1,64,64]{2,1,0:T(8,128)S(1)} %fusion.37), custom_call_target="InvertDiagBlocksLowerTriangular" | custom-call | tf_op jit(solution)/shard_map/jit(_cho_solve)/triangular_solve | solution.py:151
  281.8 0.2 convolution_bitcast_fusion.1
  281.9 0.7 fusion.38
  282.6 1.0 copy.25
  (14 shorter events, 0.2 us)
Async XLA Ops:
  7.2 1.1 copy-start
  7.2 142.6 %all-reduce.16.cloned.1.call-start = ((), (), s32[]{:S(2)}) async-start(), calls=%async_computation.1 | async-start | bytes 2097152
  15.2 5.6 %copy-start.1 = (f32[64,64]{1,0:T(8,128)S(1)}, f32[64,64]{1,0:T(8,128)}, u32[]{:S(2)}) copy-start(f32[64,64]{1,0:T(8,128)} %param.6) | copy-start | bytes 49156
  23.8 0.7 copy-start.2
  150.8 10.5 %collective-permute-start = (f32[4,3,1024]{2,1,0:T(4,128)S(1)}, f32[4,3,1024]{2,1,0:T(4,128)S(1)}, u32[]{:S(2)}, u32[]{:S(2)}) collective-permute-start(f32[4,3,1024]{2,1,0:T(4,128)S(1)} %get-tuple-element.11), channel_id=1, source_target_pairs={{0,1},{1,2},{2,3},{3,4},{4,5},{5,6},{6,7},{7,8},{8,9},{9,10},{10,1... | collective-permute-start | bytes 147464 | tf_op jit(solution)/shard_map/ppermute | solution.py:24
  154.2 9.2 %collective-permute-start.1 = (f32[4,3,1024]{2,1,0:T(4,128)S(1)}, f32[4,3,1024]{2,1,0:T(4,128)S(1)}, u32[]{:S(2)}, u32[]{:S(2)}) collective-permute-start(f32[4,3,1024]{2,1,0:T(4,128)S(1)} %get-tuple-element.12), channel_id=1, source_target_pairs={{1,0},{2,1},{3,2},{4,3},{5,4},{6,5},{7,6},{8,7},{9,8},{10,9},{11,1... | collective-permute-start | bytes 147464 | tf_op jit(solution)/shard_map/ppermute | solution.py:26
Sparse Core Ops, SparseCore 0:
  23.9 125.7 all-reduce.15
